TPU v7x, 32 devices: a whole 2x2x4 slice. The times are simulated.
32 devices in a mesh: dp: 4 (over z), seq: 8 (over y, x, core).
Axes of the slice: x: 2, y: 2, z: 4, core: 2. Of those that a mesh axis runs over, the one named last changes fastest.
Arguments:
- query_rows: bfloat16 [4, 3072, 1024], P('dp', 'seq'), may hold values from -48 to 48
- key_rows: bfloat16 [4, 3072, 1024], P('dp', 'seq'), may hold values from -8 to 8
- value_rows: bfloat16 [4, 3072, 1024], P('dp', 'seq'), may hold values from -6 to 6
- scale_end: int32 [3072], P('seq'), may hold values from 1 to 3072, as said below
- out_weight: bfloat16 [1024, 2048], replicated, may hold values from -0.8984375 to 0.8984375
- grad_out: bfloat16 [4, 3072, 2048], P('dp', 'seq'), may hold values from -1.5 to 1.5
Outputs:
- mixed_out: bfloat16 [4, 3072, 2048], P('dp', 'seq')
- out_grad: float32 [1024, 2048], P(('dp', 'seq'))
Inputs may be any that keep to these rules, and one draw needn't show every extreme that they name: scale_end is constant over each of 4 scales of consecutive tokens, equals the index one past the scale's last token (so scale_end[t] > t), never falls, and is 3072 on the last scale; the same for every image.
All inputs are finite; a program needn't handle non-finite values.
Results may differ from a plain program's by a relative error of at most 0.014.
Values may be sent and summed in bfloat16 or wider, within the bound.
No kernel may reach another device: no remote copies, remote signals or barrier semaphores. Data moves between devices by JAX's collectives and lax.ppermute only.
A program may use at most 256 MiB of HBM per device.

v0:
```python
import jax
import jax.numpy as jnp
from jax import lax
from jax.sharding import PartitionSpec as P

HEAD = 128
floor_score = -1e30


def attend_piece(carry, queries, query_end, key_piece, value_piece):
    run_max, run_sum, weighted = carry
    key_count = key_piece.shape[0]
    scores = jnp.einsum(
        "qge,kge->qgk", queries, key_piece, preferred_element_type=jnp.float32
    ) * queries.shape[2] ** (-0.5)
    positions = jnp.arange(key_count, dtype=jnp.int32)
    visible = (positions[None, :] < query_end[:, None])[:, None, :]
    masked = jnp.where(visible, scores, floor_score)
    new_max = jnp.maximum(run_max, jnp.max(masked, axis=2))
    weights = jnp.where(visible, jnp.exp(masked - new_max[:, :, None]), 0.0)
    run_sum = jnp.sum(weights, axis=2)
    product = jnp.einsum(
        "qgk,kge->qge",
        weights.astype(jnp.bfloat16),
        value_piece,
        preferred_element_type=jnp.float32,
    )
    weighted = product
    return (new_max, run_sum, weighted)


def guarded(carry, queries, query_end, key_piece, value_piece, offset):
    reach_end = jnp.max(query_end)

    def compute(state):
        return attend_piece(state, queries, query_end, key_piece, value_piece)

    def unchanged(state):
        return state

    return lax.cond(offset < reach_end, compute, unchanged, carry)


def initial_state(query_count, head_count):
    return (
        jnp.full((query_count, head_count), floor_score, jnp.float32),
        jnp.zeros((query_count, head_count), jnp.float32),
        jnp.zeros((query_count, head_count, HEAD), jnp.float32),
    )


def body(query_rows, key_rows, value_rows, scale_end, out_weight, grad_out):
    row_count = query_rows.shape[1]
    full_width = query_rows.shape[2]
    head_count = full_width // HEAD
    local_q = query_rows[0].reshape(row_count, head_count, HEAD)
    key_piece = lax.all_gather(key_rows[0], "seq", axis=0, tiled=True)
    value_piece = lax.all_gather(value_rows[0], "seq", axis=0, tiled=True)
    key_count = key_piece.shape[0]
    run_max, run_sum, weighted = guarded(
        initial_state(row_count, head_count),
        local_q,
        scale_end,
        key_piece.reshape(key_count, head_count, HEAD),
        value_piece.reshape(key_count, head_count, HEAD),
        jnp.int32(0),
    )
    attended = (weighted / run_sum[:, :, None]).astype(jnp.bfloat16).reshape(row_count, full_width)
    mixed_out = jnp.dot(attended, out_weight, preferred_element_type=jnp.float32).astype(
        jnp.bfloat16
    )[None]
    local_grad = grad_out[0]
    shares = lax.psum_scatter(
        lax.dot_general(
            attended, local_grad, (((0,), (0,)), ((), ())), preferred_element_type=jnp.float32
        ).astype(jnp.bfloat16),
        "dp",
        scatter_dimension=0,
        tiled=True,
    )
    grad_shard = lax.psum_scatter(shares, "seq", scatter_dimension=0, tiled=True).astype(
        jnp.float32
    )
    return (mixed_out, grad_shard)


def solution(mesh):
    placed = (
        P("dp", "seq", None),
        P("dp", "seq", None),
        P("dp", "seq", None),
        P("seq"),
        P(),
        P("dp", "seq", None),
    )
    return jax.shard_map(
        body,
        mesh=mesh,
        in_specs=placed,
        out_specs=(P("dp", "seq", None), P(("dp", "seq"), None)),
        check_vma=False,
    )
```

profile of v0, /device:TPU:0, one launch (start us, length us, event | category | flops | bytes accessed | tf_op | source)
XLA Modules:
  0.0 295.5 jit_solution(3256707269969613751)
XLA Ops:
  7.2 0.0 all-gather.5.cloned.1.call-start
  7.2 0.7 all-gather.5.cloned.1.call-update
  7.9 0.0 all-gather.7.cloned.1.call-start
  8.0 0.7 all-gather.7.cloned.1.call-update
  8.7 0.0 reduce-scatter.3.cloned.1.call-start
  8.7 1.3 reduce_max.18
  10.7 47.3 %all-gather.5.cloned.1.call-done = bf16[1,3072,1024]{2,1,0:T(8,128)(2,1)} async-done(((bf16[1,384,1024]{2,1,0:T(8,128)(2,1)}), bf16[1,3072,1024]{2,1,0:T(8,128)(2,1)}) %all-gather.5.cloned.1.call-update) | async-done | bytes 6291472 | tf_op jit(solution)/shard_map/all_gather | solution.py:57
  58.0 47.3 %all-gather.7.cloned.1.call-done = bf16[1,3072,1024]{2,1,0:T(8,128)(2,1)} async-done(((bf16[1,384,1024]{2,1,0:T(8,128)(2,1)}), bf16[1,3072,1024]{2,1,0:T(8,128)(2,1)}) %all-gather.7.cloned.1.call-update) | async-done | bytes 6291472 | tf_op jit(solution)/shard_map/all_gather | solution.py:58
  105.3 60.2 %conditional.1 = (f32[384,8]{0,1:T(8,128)S(1)}, f32[384,8,128]{0,2,1:T(8,128)S(1)}) conditional(s32[]{:T(128)} %convert_element_type.18, () %tuple.16, (s32[384]{0:T(512)}, bf16[3072,1024]{1,0:T(8,128)(2,1)}, bf16[1,384,1024]{2,1,0:T(8,128)(2,1)}, bf16[3072,1024]{1,0:T(8,128)(2,1)}) %tuple.33), branch_computations={%region_1.0_spmd, %region_2.5_spmd} | conditional | flops 4955698176 | bytes 137700880 | solution.py:41
  105.3 1.3 copy.30
  106.6 1.6 iota_compare_fusion
  108.2 17.6 %fusion = (f32[384,8]{0,1:T(8,128)S(1)}, f32[8,3072,384]{2,1,0:T(8,128)}) fusion(pred[384,3072]{0,1:T(8,128)(4,1)S(1)} %iota_compare_fusion, bf16[384,8,128]{2,1,0:T(8,128)(2,1)S(1)} %bitcast.48, bf16[3072,1024]{1,0:T(8,128)(2,1)} %get-tuple-element.12), kind=kOutput, calls=%fused_computation.2 | convolution fusion | flops 2444227584 | bytes 46018560 | tf_op jit(solution)/shard_map/cond/branch_1_fun/qge,kge->qgk/dot_general | solution.py:13
  125.8 21.0 %fusion.11 = f32[384,8,128]{2,0,1:T(8,128)} fusion(f32[8,3072,384]{2,1,0:T(8,128)} %get-tuple-element.25, f32[384,8]{0,1:T(8,128)S(1)} %broadcast_maximum_fusion, pred[384,3072]{0,1:T(8,128)(4,1)S(1)} %iota_compare_fusion, bf16[3072,1024]{1,0:T(8,128)(2,1)} %get-tuple-element.14), kind=kOutput, calls=%fused_computation.13 | convolution fusion | flops 2463105024 | bytes 46804992 | tf_op jit(solution)/shard_map/cond/branch_1_fun/qgk,kge->qge/dot_general | solution.py:22
  146.8 16.6 %fusion.2 = f32[384,8]{0,1:T(8,128)S(1)} fusion(f32[8,3072,384]{2,1,0:T(8,128)} %get-tuple-element.25, f32[384,8]{0,1:T(8,128)S(1)} %broadcast_maximum_fusion, pred[384,3072]{0,1:T(8,128)(4,1)S(1)} %iota_compare_fusion), kind=kLoop, calls=%fused_computation.4 | loop fusion | flops 47182848 | bytes 38952960 | tf_op jit(solution)/shard_map/cond/branch_1_fun/reduce_sum | solution.py:21
  163.4 1.9 copy.27
  165.5 0.1 divide_convert_fusion
  165.7 0.9 copy-done.1
  166.6 4.3 %convolution_convert_fusion = bf16[1024,2048]{1,0:T(8,128)(2,1)} fusion(bf16[384,1024]{0,1:T(8,128)(2,1)S(1)} %bitcast.49, bf16[1,384,2048]{2,1,0:T(8,128)(2,1)S(1)} %copy-done), kind=kOutput, calls=%fused_computation.19 | convolution fusion | flops 1612709888 | bytes 6553600 | tf_op jit(solution)/shard_map/dot_general | solution.py:74
  170.9 0.0 reduce-scatter.3.cloned.1.call-update
  170.9 0.0 reduce-scatter.5.cloned.1.call-start
  170.9 76.9 %reduce-scatter.3.cloned.1.call-done = bf16[256,2048]{1,0:T(8,128)(2,1)} async-done(((bf16[1024,2048]{1,0:T(8,128)(2,1)}), bf16[256,2048]{1,0:T(8,128)(2,1)}) %reduce-scatter.3.cloned.1.call-update) | async-done | bytes 1048592 | tf_op jit(solution)/shard_map/reduce_scatter | solution.py:73
  247.8 5.4 %fusion.20 = bf16[1,384,2048]{2,1,0:T(8,128)(2,1)} fusion(bf16[384,1024]{0,1:T(8,128)(2,1)} %bitcast.50, bf16[1024,2048]{1,0:T(8,128)(2,1)} %param.12), kind=kOutput, calls=%fused_computation.21 | convolution fusion | flops 1611399168 | bytes 6553600 | tf_op jit(solution)/shard_map/dot_general | solution.py:69
  253.2 34.1 %reduce-scatter.5.cloned.1.call-done = bf16[32,2048]{1,0:T(8,128)(2,1)} async-done(((bf16[256,2048]{1,0:T(8,128)(2,1)}), bf16[32,2048]{1,0:T(8,128)(2,1)}) %reduce-scatter.5.cloned.1.call-update) | async-done | bytes 131088 | tf_op jit(solution)/shard_map/reduce_scatter | solution.py:81
  287.3 1.6 convert_element_type.22
  (5 shorter events, 0.0 us)
Async XLA Ops:
  7.2 159.4 %copy-start = (bf16[1,384,2048]{2,1,0:T(8,128)(2,1)S(1)}, bf16[1,384,2048]{2,1,0:T(8,128)(2,1)}, u32[]{:S(2)}) copy-start(bf16[1,384,2048]{2,1,0:T(8,128)(2,1)} %param.13) | copy-start | bytes 4718596
  7.2 50.8 %all-gather.5.cloned.1.call-start = ((), (), s32[]{:S(2)}) async-start(), calls=%async_computation.4 | async-start | bytes 7077888 | tf_op jit(solution)/shard_map/all_gather | solution.py:57
  7.9 97.4 %all-gather.7.cloned.1.call-start = ((), (), s32[]{:S(2)}) async-start(), calls=%async_computation.5 | async-start | bytes 7077888 | tf_op jit(solution)/shard_map/all_gather | solution.py:58
  8.7 239.1 %reduce-scatter.3.cloned.1.call-start = ((), (), s32[]{:S(2)}) async-start(), calls=%async_computation.2 | async-start | bytes 5242880 | tf_op jit(solution)/shard_map/reduce_scatter | solution.py:73
  165.6 0.9 copy-start.1
  170.9 116.5 %reduce-scatter.5.cloned.1.call-start = ((), (), s32[]{:S(2)}) async-start(), calls=%async_computation.3 | async-start | bytes 1179648 | tf_op jit(solution)/shard_map/reduce_scatter | solution.py:81
Sparse Core Ops, SparseCore 0:
  9.9 48.1 all-gather.4
  59.9 45.3 all-gather.6
  171.0 76.7 reduce-scatter.2
  250.8 36.4 reduce-scatter.4
where the time goes:
time: 296 us; the launch traced here: 295 us
  waiting for transfers between devices  207 us (70%)
  matrix products  48.3 us (16%)
  other arithmetic  21.3 us (7%)
  between operations  14.4 us (5%)
  local copies, waits for them, and re-layouts  4.09 us (1%)
    reduce_scatter x1, waiting for transfers between devices, body(): lax.psum_scatter(lax.dot_general(attended, local_grad, (((0,), (0,)), (()...  76.9 us
    all_gather x1, waiting for transfers between devices, body(): key_piece = lax.all_gather(key_rows[0], 'seq', axis=0, tiled=True)  47.3 us
    all_gather x1, waiting for transfers between devices, body(): value_piece = lax.all_gather(value_rows[0], 'seq', axis=0, tiled=True)  47.3 us
    reduce_scatter x1, waiting for transfers between devices, body(): lax.psum_scatter(shares, 'seq', scatter_dimension=0, tiled=True)  34.1 us
    dot_general x1, matrix products, attend_piece(): jnp.einsum('qgk,kge->qge', weights.astype(jnp.bfloat16), value_piece, pre...  21 us
    dot_general x1, matrix products, attend_piece(): jnp.einsum('qge,kge->qgk', queries, key_piece, preferred_element_type=jnp...  17.6 us
    reduce_sum x1, other arithmetic, attend_piece(): run_sum = jnp.sum(weights, axis=2)  16.6 us
  transfers between devices with their start and end apart: 4, of which 4 were waited for; matrix products, arithmetic and copies ran while one was open for 2% of the time, Pallas kernels for 0%

commit v1 on v0

--- a/solution.py
+++ b/solution.py
@@ -54,7 +54,9 @@
     full_width = query_rows.shape[2]
     head_count = full_width // HEAD
     local_q = query_rows[0].reshape(row_count, head_count, HEAD)
-    key_piece = lax.all_gather(key_rows[0], "seq", axis=0, tiled=True)
+    key_piece = jnp.concatenate(
+        lax.all_to_all(jnp.stack([key_rows[0]] * lax.axis_size("seq")), "seq", 0, 0), axis=0
+    )
     value_piece = lax.all_gather(value_rows[0], "seq", axis=0, tiled=True)
     key_count = key_piece.shape[0]
     run_max, run_sum, weighted = guarded(

time: 296 us -> 313 us (1.057)
  local copies, waits for them, and re-layouts: 4.09 us -> 14.6 us
  starting transfers between devices: 0.16 us -> 5.45 us
    all_to_all x0 -> x1, waiting for transfers between devices: none -> 95.8 us  [body(): lax.all_to_all(jnp.stack([key_rows[0]] * lax.axis_size('seq')), 'seq', 0, 0)]
    all_gather x1 -> x0, waiting for transfers between devices: 47.3 us -> none  [body(): key_piece = lax.all_gather(key_rows[0], 'seq', axis=0, tiled=True)]
    all_gather x1, waiting for transfers between devices: 47.3 us -> 0.01 us  [body(): value_piece = lax.all_gather(value_rows[0], 'seq', axis=0, tiled=True)]
    cond x1 -> x4, local copies, waits for them, and re-layouts: 1.3 us -> 7.24 us
    all_to_all x0 -> x1, starting transfers between devices: none -> 5.33 us  [body(): lax.all_to_all(jnp.stack([key_rows[0]] * lax.axis_size('seq')), 'seq', 0, 0)]
    another operation x0 -> x1, local copies, waits for them, and re-layouts: none -> 4.59 us  [body(): jnp.stack([key_rows[0]] * lax.axis_size('seq'))]
  transfers between devices with their start and end apart: 4 -> 4, of which waited for: 4 -> 3; matrix products, arithmetic and copies ran while one was open for 2% -> 3% of each run, Pallas kernels for 0% -> 0%
where the time goes in v1:
time: 313 us; the launch traced here: 312 us
  waiting for transfers between devices  209 us (67%)
  matrix products  48.6 us (16%)
  other arithmetic  19.9 us (6%)
  local copies, waits for them, and re-layouts  14.6 us (5%)
  between operations  14.4 us (5%)
  starting transfers between devices  5.45 us (2%)
    all_to_all x1, waiting for transfers between devices, body(): lax.all_to_all(jnp.stack([key_rows[0]] * lax.axis_size('seq')), 'seq', 0, 0)  95.8 us
    reduce_scatter x1, waiting for transfers between devices, body(): lax.psum_scatter(lax.dot_general(attended, local_grad, (((0,), (0,)), (()...  78.1 us
    reduce_scatter x1, waiting for transfers between devices, body(): lax.psum_scatter(shares, 'seq', scatter_dimension=0, tiled=True)  34.3 us
    dot_general x1, matrix products, attend_piece(): jnp.einsum('qgk,kge->qge', weights.astype(jnp.bfloat16), value_piece, pre...  21.1 us
    dot_general x1, matrix products, attend_piece(): jnp.einsum('qge,kge->qgk', queries, key_piece, preferred_element_type=jnp...  17.8 us
    reduce_sum x1, other arithmetic, attend_piece(): run_sum = jnp.sum(weights, axis=2)  16.6 us
    cond x4, local copies, waits for them, and re-layouts  7.24 us
  transfers between devices with their start and end apart: 4, of which 3 were waited for; matrix products, arithmetic and copies ran while one was open for 3% of the time, Pallas kernels for 0%

profile of v1, /device:TPU:0, one launch (start us, length us, event | category | flops | bytes accessed | tf_op | source)
XLA Modules:
  0.0 312.1 jit_solution(12768785032183907030)
XLA Ops:
  7.2 0.0 all-gather.3.cloned.1.call-start
  7.2 0.7 all-gather.3.cloned.1.call-update
  7.9 4.6 %stack.3 = bf16[8,384,1024]{2,1,0:T(8,128)(2,1)} broadcast(bf16[384,1024]{1,0:T(8,128)(2,1)} %bitcast.42), dimensions={1,2} | broadcast | bytes 7077888 | tf_op jit(solution)/shard_map/stack | solution.py:58
  12.5 5.3 %all-to-all-start = ((bf16[8,384,1024]{2,1,0:T(8,128)(2,1)}), bf16[8,384,1024]{2,1,0:T(8,128)(2,1)}, u32[]{:S(2)}, u32[]{:S(2)}) async-start(bf16[8,384,1024]{2,1,0:T(8,128)(2,1)} %stack.3), calls=%async_computation | async-start | bytes 12582912 | tf_op jit(solution)/shard_map/all_to_all | solution.py:58
  17.8 0.0 reduce-scatter.3.cloned.1.call-start
  17.9 0.6 reduce_max.18
  19.2 95.8 %all-to-all-done = bf16[8,384,1024]{2,1,0:T(8,128)(2,1)} async-done(((bf16[8,384,1024]{2,1,0:T(8,128)(2,1)}), bf16[8,384,1024]{2,1,0:T(8,128)(2,1)}, u32[]{:S(2)}, u32[]{:S(2)}) %all-to-all-start) | async-done | bytes 6291488 | tf_op jit(solution)/shard_map/all_to_all | solution.py:58
  114.9 65.7 %conditional.1 = (f32[384,8]{0,1:T(8,128)S(1)}, f32[384,8,128]{0,2,1:T(8,128)S(1)}) conditional(s32[]{:T(128)} %convert_element_type.18, () %tuple.16, (s32[384]{0:T(512)S(1)}, bf16[8,384,1024]{2,1,0:T(8,128)(2,1)}, bf16[1,384,1024]{2,1,0:T(8,128)(2,1)}, bf16[3072,1024]{1,0:T(8,128)(2,1)}) %tuple.31), branch_computations={%region_1.0_spmd, %region_2.5_spmd} | conditional | flops 4955698176 | bytes 153429552 | solution.py:41
  115.0 7.1 %copy.29 = bf16[384,8,8,128]{3,2,1,0:T(8,128)(2,1)} copy(bf16[384,8,8,128]{3,1,2,0:T(8,128)(2,1)} %bitcast.10) | data formatting | bytes 12582912 | tf_op jit(solution)/shard_map/cond
  122.0 0.2 copy.30
  122.2 0.9 iota_compare_fusion
  123.1 17.8 %fusion = (f32[384,8]{0,1:T(8,128)S(1)}, f32[8,3072,384]{2,1,0:T(8,128)}) fusion(pred[384,3072]{0,1:T(8,128)(4,1)S(1)} %iota_compare_fusion, bf16[384,8,128]{2,1,0:T(8,128)(2,1)S(1)} %bitcast.44, bf16[3072,8,128]{2,1,0:T(8,128)(2,1)} %bitcast.41), kind=kOutput, calls=%fused_computation.2 | convolution fusion | flops 2444227584 | bytes 46018560 | tf_op jit(solution)/shard_map/cond/branch_1_fun/qge,kge->qgk/dot_general | solution.py:13
  140.9 21.1 %fusion.10 = f32[384,8,128]{2,0,1:T(8,128)} fusion(f32[8,3072,384]{2,1,0:T(8,128)} %get-tuple-element.25, f32[384,8]{0,1:T(8,128)S(1)} %broadcast_maximum_fusion, pred[384,3072]{0,1:T(8,128)(4,1)S(1)} %iota_compare_fusion, bf16[3072,1024]{1,0:T(8,128)(2,1)} %get-tuple-element.14), kind=kOutput, calls=%fused_computation.12 | convolution fusion | flops 2463105024 | bytes 46804992 | tf_op jit(solution)/shard_map/cond/branch_1_fun/qgk,kge->qge/dot_general | solution.py:22
  162.0 16.6 %fusion.2 = f32[384,8]{0,1:T(8,128)S(1)} fusion(f32[8,3072,384]{2,1,0:T(8,128)} %get-tuple-element.25, f32[384,8]{0,1:T(8,128)S(1)} %broadcast_maximum_fusion, pred[384,3072]{0,1:T(8,128)(4,1)S(1)} %iota_compare_fusion), kind=kLoop, calls=%fused_computation.4 | loop fusion | flops 47182848 | bytes 38952960 | tf_op jit(solution)/shard_map/cond/branch_1_fun/reduce_sum | solution.py:21
  178.6 1.9 copy.27
  180.7 0.1 divide_convert_fusion
  180.9 0.9 copy-done.2
  181.8 4.3 %convolution_convert_fusion = bf16[1024,2048]{1,0:T(8,128)(2,1)} fusion(bf16[384,1024]{0,1:T(8,128)(2,1)S(1)} %bitcast.45, bf16[1,384,2048]{2,1,0:T(8,128)(2,1)S(1)} %copy-done), kind=kOutput, calls=%fused_computation.18 | convolution fusion | flops 1612709888 | bytes 6553600 | tf_op jit(solution)/shard_map/dot_general | solution.py:76
  186.1 0.0 reduce-scatter.3.cloned.1.call-update
  186.1 0.0 reduce-scatter.5.cloned.1.call-start
  186.2 78.1 %reduce-scatter.3.cloned.1.call-done = bf16[256,2048]{1,0:T(8,128)(2,1)} async-done(((bf16[1024,2048]{1,0:T(8,128)(2,1)}), bf16[256,2048]{1,0:T(8,128)(2,1)}) %reduce-scatter.3.cloned.1.call-update) | async-done | bytes 1048592 | tf_op jit(solution)/shard_map/reduce_scatter | solution.py:75
  264.3 5.4 %fusion.19 = bf16[1,384,2048]{2,1,0:T(8,128)(2,1)} fusion(bf16[384,1024]{0,1:T(8,128)(2,1)} %bitcast.46, bf16[1024,2048]{1,0:T(8,128)(2,1)} %param.12), kind=kOutput, calls=%fused_computation.20 | convolution fusion | flops 1611399168 | bytes 6553600 | tf_op jit(solution)/shard_map/dot_general | solution.py:71
  269.7 34.3 %reduce-scatter.5.cloned.1.call-done = bf16[32,2048]{1,0:T(8,128)(2,1)} async-done(((bf16[256,2048]{1,0:T(8,128)(2,1)}), bf16[32,2048]{1,0:T(8,128)(2,1)}) %reduce-scatter.5.cloned.1.call-update) | async-done | bytes 131088 | tf_op jit(solution)/shard_map/reduce_scatter | solution.py:83
  303.9 1.6 convert_element_type.22
  (10 shorter events, 0.0 us)
Async XLA Ops:
  7.2 174.6 %copy-start = (bf16[1,384,2048]{2,1,0:T(8,128)(2,1)S(1)}, bf16[1,384,2048]{2,1,0:T(8,128)(2,1)}, u32[]{:S(2)}) copy-start(bf16[1,384,2048]{2,1,0:T(8,128)(2,1)} %param.13) | copy-start | bytes 4718596
  7.2 107.8 %all-gather.3.cloned.1.call-start = ((), (), s32[]{:S(2)}) async-start(), calls=%async_computation.5 | async-start | bytes 7077888 | tf_op jit(solution)/shard_map/all_gather | solution.py:60
  12.5 5.4 %copy-start.3 = (s32[384]{0:T(512)S(1)}, s32[384]{0:T(512)}, u32[]{:S(2)}) copy-start(s32[384]{0:T(512)} %param.11) | copy-start | bytes 4612
  12.5 102.4 %all-to-all-start = ((bf16[8,384,1024]{2,1,0:T(8,128)(2,1)}), bf16[8,384,1024]{2,1,0:T(8,128)(2,1)}, u32[]{:S(2)}, u32[]{:S(2)}) async-start(bf16[8,384,1024]{2,1,0:T(8,128)(2,1)} %stack.3), calls=%async_computation | async-start | bytes 12582912 | tf_op jit(solution)/shard_map/all_to_all | solution.py:58
  17.8 246.4 %reduce-scatter.3.cloned.1.call-start = ((), (), s32[]{:S(2)}) async-start(), calls=%async_computation.3 | async-start | bytes 5242880 | tf_op jit(solution)/shard_map/reduce_scatter | solution.py:75
  114.9 7.1 %copy-start.1 = (bf16[1,384,1024]{2,1,0:T(8,128)(2,1)S(1)}, bf16[1,384,1024]{2,1,0:T(8,128)(2,1)}, u32[]{:S(2)}) copy-start(bf16[1,384,1024]{2,1,0:T(8,128)(2,1)} %get-tuple-element.22) | copy-start | bytes 2359300 | tf_op jit(solution)/shard_map/cond
  180.8 0.9 copy-start.2
  186.1 117.8 %reduce-scatter.5.cloned.1.call-start = ((), (), s32[]{:S(2)}) async-start(), calls=%async_computation.4 | async-start | bytes 1179648 | tf_op jit(solution)/shard_map/reduce_scatter | solution.py:83
Sparse Core Ops, SparseCore 0:
  9.9 89.2 all-gather.2
  186.2 77.9 reduce-scatter.2
  267.4 36.4 reduce-scatter.4
